TPU v7x, 512 devices: a whole 4x8x8 slice. The times are simulated.
512 devices in a mesh: row: 32 (over z, y_hi), col: 16 (over x, y_lo, core).
Axes of the slice: x: 4, y: 8 (y_hi: 4, y_lo: 2; y = y_hi * 2 + y_lo), z: 8, core: 2. Of those that a mesh axis runs over, the one named last changes fastest.
Arguments:
- vectors: float32 [16384, 2048], P('row', 'col'), may hold values from -6 to 6
- reflectors: float32 [32, 1024, 512], P('row', 'col'), may hold values from -2 to 2
- factors: float32 [32, 512, 512], P('row', 'col'), may hold values from -2 to 2
Outputs:
- transformed: float32 [16384, 2048], P('row', 'col')
All inputs are finite; a program needn't handle non-finite values.
Results may differ from a plain program's by a relative error of at most 0.0003.
Values sent between devices are 32-bit elements; how exact they have to be, the bound alone decides.
No kernel may reach another device: no remote copies, remote signals or barrier semaphores. Data moves between devices by JAX's collectives and lax.ppermute only.
A program may use at most 64 MiB of HBM per device.

v0:
```python
import jax
import jax.numpy as jnp
from jax import lax
from jax.sharding import Mesh
from jax.sharding import PartitionSpec as P

ROW = ("z", "h")
COL = ("x", "l", "c")


def dot(a, b, da, db):
    return lax.dot_general(
        a, b, (((da,), (db,)), ((), ())), precision=lax.Precision.HIGH, preferred_element_type=jnp.float32
    )


def spread(part, axes):
    count = lax.axis_size(axes)
    return lax.all_to_all(jnp.broadcast_to(part[None], (count, *part.shape)), axes, 0, 0)


def both_halves(own, core, dim):
    other = lax.ppermute(own, "c", [(0, 1), (1, 0)])
    first = jnp.where(core == 0, own, other)
    second = jnp.where(core == 0, other, own)
    return jnp.stack([first, second], axis=dim)


def pick(choices, which):
    value = choices[-1]
    for k in reversed(range(len(choices) - 1)):
        if choices[k] is not value:
            value = jnp.where(which == k, choices[k], value)
    return value


def transformed(vectors, reflectors, factors):
    planes, rows = lax.axis_size("z"), lax.axis_size("h")
    core, place = lax.axis_index("c"), lax.axis_index("h")
    band, strip = factors.shape[2], reflectors.shape[1]
    part = spread(jnp.concatenate([reflectors[0], factors[0]], axis=0), ("x", "l"))
    blocks = both_halves(part, core, 1)
    shaped = blocks[:, :, :strip].reshape(2 * band, band)
    triangle = blocks[:, :, strip:].reshape(band, band)
    upper, lower = shaped[:band], shaped[band:]
    chips = lax.axis_size(("x", "l"))
    height = band // (2 * chips)
    here = core * chips + lax.axis_index(("x", "l"))
    own = -dot(dot(lax.dynamic_slice_in_dim(upper, here * height, height, 0), triangle, 1, 0), lower, 1, 1)
    shards = spread(own, "h")
    reach = dot(triangle, lower, 1, 1)
    inner = dot(dot(vectors, upper, 0, 0), triangle, 1, 1)
    edge = vectors.T - dot(inner, upper, 1, 1)
    width = edge.shape[0] // rows
    slices, edges = edge.reshape(rows, width, band), []
    for s in range(rows):
        piece = lax.dynamic_index_in_dim(slices, (place - s) % rows, 0, keepdims=False)
        above = [(k, (k - s) % rows) for k in range(rows)]
        edges.append(lax.ppermute(piece, "h", above) if s else piece)
    edges = [pick([edges[(k - h) % rows] for h in range(rows)], place) for k in range(rows)]
    coupling = lax.optimization_barrier(-dot(upper, reach, 1, 0))
    others = [jnp.where(place <= k, shards[k + 1], shards[k]) for k in range(rows - 1)]
    part = spread(jnp.stack(others), ("x", "l"))
    halves = both_halves(part, core, 0).transpose(2, 0, 1, 3, 4).reshape(rows - 1, band, band)
    couplings = [
        pick([halves[k - 1] if k > h else coupling if k == h else halves[k] for h in range(rows)], place)
        for k in range(rows)
    ]
    count = planes * rows
    down = [(k, k + 1) for k in range(count - 1)]
    pull = dot(lower, reach, 1, 0)
    pull = lax.dynamic_slice_in_dim(pull, core * (band // 2), band // 2, 0)
    extra = jnp.concatenate([pull, dot(inner, lower, 1, 1)])
    extra = lax.ppermute(extra, ROW, down)
    pull, fixed = both_halves(extra[: band // 2], core, 0).reshape(band, band), extra[band // 2 :]
    total, bottom = couplings[rows - 1], edges[rows - 1]
    for k in reversed(range(rows - 1)):
        bottom = edges[k] + dot(bottom, couplings[k], 1, 1)
        total = dot(couplings[k], total, 1, 0)
    top, below = bottom, jnp.zeros_like(bottom)
    for k in reversed(range(1, planes)):
        came = lax.ppermute(top, "z", [(k, k - 1)])
        top = top + dot(came, total, 1, 1)
        below = below + came
    tops = [below]
    for k in reversed(range(1, rows)):
        tops.insert(0, edges[k] + dot(tops[0], couplings[k], 1, 1))
    mine = jnp.stack([top, *tops[:-1]])
    mine = lax.all_to_all(mine, "h", 0, 0).reshape(rows * width, band)
    return mine.T - dot(pull, mine, 1, 1) - fixed.T


def solution(mesh):
    split = Mesh(mesh.devices.reshape(8, 4, 4, 2, 2), ROW + COL)
    return jax.shard_map(
        transformed,
        mesh=split,
        in_specs=(P(ROW, COL), P(ROW, COL, None), P(ROW, COL, None)),
        out_specs=P(ROW, COL),
        check_vma=False,
    )
```

profile of v0, /device:TPU:258, one launch (start us, length us, event | category | flops | bytes accessed | tf_op | source)
XLA Modules:
  0.0 185.9 jit_solution(2104975007292487597)
XLA Ops:
  1.2 25.3 %all_to_all.20 = f32[8,96,512]{2,1,0:T(8,128)S(1)} all-to-all(f32[8,96,512]{2,1,0:T(8,128)S(1)} %broadcast_in_dim.6), channel_id=1, replica_groups=mesh['z'=8,'h'=4,'x'=4,'l'=2,'c'=2] {'x','l'}, dimensions={0} | all-to-all | bytes 3145728 | tf_op jit(solution)/shard_map/all_to_all | solution.py:19
  26.5 1.9 %collective-permute-start = (f32[8,96,512]{2,1,0:T(8,128)S(1)}, f32[8,96,512]{2,1,0:T(8,128)}, u32[]{:S(2)}, u32[]{:S(2)}) collective-permute-start(f32[8,96,512]{2,1,0:T(8,128)S(1)} %all_to_all.20), channel_id=1, source_target_pairs={{0,1},{1,0},{2,3},{3,2},{4,5},{5,4},{6,7},{7,6},{8,9},{9,8},{10,11... | collective-permute-start | bytes 4718600 | tf_op jit(solution)/shard_map/ppermute | solution.py:23
  28.4 3.5 %collective-permute-done = f32[8,96,512]{2,1,0:T(8,128)} collective-permute-done((f32[8,96,512]{2,1,0:T(8,128)S(1)}, f32[8,96,512]{2,1,0:T(8,128)}, u32[]{:S(2)}, u32[]{:S(2)}) %collective-permute-start) | collective-permute-done | bytes 1572896 | tf_op jit(solution)/shard_map/ppermute | solution.py:23
  31.9 1.8 select_bitcast_fusion.2
  35.6 6.2 %all-to-all-start.1 = ((f32[4,32,512]{2,1,0:T(8,128)}), f32[4,32,512]{2,1,0:T(8,128)S(1)}, u32[]{:S(2)}, u32[]{:S(2)}) async-start(f32[4,32,512]{2,1,0:T(8,128)} %broadcast_in_dim.7), calls=%async_computation.1 | async-start | bytes 524288 | tf_op jit(solution)/shard_map/all_to_all | solution.py:19
  41.8 11.1 %all-to-all-done.1 = f32[4,32,512]{2,1,0:T(8,128)S(1)} async-done(((f32[4,32,512]{2,1,0:T(8,128)}), f32[4,32,512]{2,1,0:T(8,128)S(1)}, u32[]{:S(2)}, u32[]{:S(2)}) %all-to-all-start.1) | async-done | bytes 262176 | tf_op jit(solution)/shard_map/all_to_all | solution.py:19
  53.0 1.3 broadcast_in_dim.8
  54.3 5.7 %all-to-all-start.2 = ((f32[8,3,32,512]{3,2,1,0:T(8,128)}), f32[8,3,32,512]{3,2,1,0:T(8,128)}, u32[]{:S(2)}, u32[]{:S(2)}) async-start(f32[8,3,32,512]{3,2,1,0:T(8,128)} %broadcast_in_dim.8), calls=%async_computation.2 | async-start | bytes 3145728 | tf_op jit(solution)/shard_map/all_to_all | solution.py:19
  61.1 2.7 %fusion.21 = f32[512,128]{1,0:T(8,128)} fusion(f32[512,512]{1,0:T(8,128)S(1)} %bitcast.129, f32[512,128]{1,0:T(8,128)} %param.3), kind=kOutput, calls=%fused_computation.72 | convolution fusion | flops 201326592 | bytes 1572864 | tf_op jit(solution)/shard_map/dot_general | solution.py:12
  63.8 13.8 %all-to-all-done.2 = f32[8,3,32,512]{3,2,1,0:T(8,128)} async-done(((f32[8,3,32,512]{3,2,1,0:T(8,128)}), f32[8,3,32,512]{3,2,1,0:T(8,128)}, u32[]{:S(2)}, u32[]{:S(2)}) %all-to-all-start.2) | async-done | bytes 1572896 | tf_op jit(solution)/shard_map/all_to_all | solution.py:19
  77.6 1.9 %collective-permute-start.4 = (f32[8,3,32,512]{3,2,1,0:T(8,128)}, f32[8,3,32,512]{3,2,1,0:T(8,128)S(1)}, u32[]{:S(2)}, u32[]{:S(2)}) collective-permute-start(f32[8,3,32,512]{3,2,1,0:T(8,128)} %all-to-all-done.2), channel_id=1, source_target_pairs={{0,1},{1,0},{2,3},{3,2},{4,5},{5,4},{6,7},{7,6},{8,9},{9,8},{10,11... | collective-permute-start | bytes 4718600 | tf_op jit(solution)/shard_map/ppermute | solution.py:23
  79.5 1.6 fusion.22
  81.9 6.3 %collective-permute-start.2 = (f32[32,512]{1,0:T(8,128)S(1)}, f32[32,512]{1,0:T(8,128)S(1)}, u32[]{:S(2)}, u32[]{:S(2)}) collective-permute-start(f32[32,512]{1,0:T(8,128)S(1)} %get-tuple-element.27), channel_id=1, source_target_pairs={{0,32},{16,48},{32,0},{48,16},{1,33},{17,49},{33,1},{49,17},{2,34}... | collective-permute-start | bytes 196616 | tf_op jit(solution)/shard_map/ppermute | solution.py:59
  88.2 5.5 %collective-permute-start.3 = (f32[32,512]{1,0:T(8,128)S(1)}, f32[32,512]{1,0:T(8,128)S(1)}, u32[]{:S(2)}, u32[]{:S(2)}) collective-permute-start(f32[32,512]{1,0:T(8,128)S(1)} %get-tuple-element.26), channel_id=1, source_target_pairs={{0,48},{16,0},{32,16},{48,32},{1,49},{17,1},{33,17},{49,33},{2,50}... | collective-permute-start | bytes 196616 | tf_op jit(solution)/shard_map/ppermute | solution.py:59
  93.7 1.9 %collective-permute-start.1 = (f32[32,512]{1,0:T(8,128)S(1)}, f32[32,512]{1,0:T(8,128)S(1)}, u32[]{:S(2)}, u32[]{:S(2)}) collective-permute-start(f32[32,512]{1,0:T(8,128)S(1)} %get-tuple-element.28), channel_id=1, source_target_pairs={{0,16},{16,32},{32,48},{48,0},{1,17},{17,33},{33,49},{49,1},{2,18}... | collective-permute-start | bytes 196616 | tf_op jit(solution)/shard_map/ppermute | solution.py:59
  98.7 3.9 %collective-permute-done.1 = f32[32,512]{1,0:T(8,128)S(1)} collective-permute-done((f32[32,512]{1,0:T(8,128)S(1)}, f32[32,512]{1,0:T(8,128)S(1)}, u32[]{:S(2)}, u32[]{:S(2)}) %collective-permute-start.1) | collective-permute-done | bytes 65568 | tf_op jit(solution)/shard_map/ppermute | solution.py:59
  102.6 1.8 select_bitcast_fusion.1
  115.3 9.5 %collective-permute-done.7 = f32[32,512]{1,0:T(8,128)S(1)} collective-permute-done((f32[32,512]{1,0:T(8,128)S(1)}, f32[32,512]{1,0:T(8,128)S(1)}, u32[]{:S(2)}, u32[]{:S(2)}) %collective-permute-start.7) | collective-permute-done | bytes 65568 | tf_op jit(solution)/shard_map/ppermute | solution.py:82
  125.4 1.3 collective-permute-start.8
  126.8 1.9 %collective-permute-start.12 = (f32[384,512]{1,0:T(8,128)S(1)}, f32[384,512]{1,0:T(8,128)S(1)}, u32[]{:S(2)}, u32[]{:S(2)}) collective-permute-start(f32[384,512]{1,0:T(8,128)S(1)} %pad_maximum_fusion.2), channel_id=1, source_target_pairs={{0,16},{16,32},{32,48},{48,64},{64,80},{80,96},{96,112},{112,128},... | collective-permute-start | bytes 2359304 | tf_op jit(solution)/shard_map/ppermute | solution.py:74
  132.5 32.2 %collective-permute-done.12 = f32[384,512]{1,0:T(8,128)S(1)} collective-permute-done((f32[384,512]{1,0:T(8,128)S(1)}, f32[384,512]{1,0:T(8,128)S(1)}, u32[]{:S(2)}, u32[]{:S(2)}) %collective-permute-start.12) | collective-permute-done | bytes 786464 | tf_op jit(solution)/shard_map/ppermute | solution.py:74
  164.8 1.9 %collective-permute-start.13 = (f32[256,512]{1,0:T(8,128)S(1)}, f32[256,512]{1,0:T(8,128)S(1)}, u32[]{:S(2)}, u32[]{:S(2)}) collective-permute-start(f32[256,512]{1,0:T(8,128)S(1)} %slice.84), channel_id=1, source_target_pairs={{0,1},{1,0},{2,3},{3,2},{4,5},{5,4},{6,7},{7,6},{8,9},{9,8},{10,11... | collective-permute-start | bytes 1572872 | tf_op jit(solution)/shard_map/ppermute | solution.py:23
  169.8 3.4 %all-to-all-start.3 = ((f32[4,32,512]{2,1,0:T(8,128)}), f32[4,32,512]{2,1,0:T(8,128)S(1)}, u32[]{:S(2)}, u32[]{:S(2)}) async-start(f32[4,32,512]{2,1,0:T(8,128)} %pad_maximum_fusion.3), calls=%async_computation.3 | async-start | bytes 524288 | tf_op jit(solution)/shard_map/all_to_all | solution.py:89
  173.4 11.0 %all-to-all-done.3 = f32[4,32,512]{2,1,0:T(8,128)S(1)} async-done(((f32[4,32,512]{2,1,0:T(8,128)}), f32[4,32,512]{2,1,0:T(8,128)S(1)}, u32[]{:S(2)}, u32[]{:S(2)}) %all-to-all-start.3) | async-done | bytes 262176 | tf_op jit(solution)/shard_map/all_to_all | solution.py:89
  (60 shorter events, 27.8 us)
Async XLA Ops:
  26.5 5.4 %collective-permute-start = (f32[8,96,512]{2,1,0:T(8,128)S(1)}, f32[8,96,512]{2,1,0:T(8,128)}, u32[]{:S(2)}, u32[]{:S(2)}) collective-permute-start(f32[8,96,512]{2,1,0:T(8,128)S(1)} %all_to_all.20), channel_id=1, source_target_pairs={{0,1},{1,0},{2,3},{3,2},{4,5},{5,4},{6,7},{7,6},{8,9},{9,8},{10,11... | collective-permute-start | bytes 4718600 | tf_op jit(solution)/shard_map/ppermute | solution.py:23
  35.6 17.3 %all-to-all-start.1 = ((f32[4,32,512]{2,1,0:T(8,128)}), f32[4,32,512]{2,1,0:T(8,128)S(1)}, u32[]{:S(2)}, u32[]{:S(2)}) async-start(f32[4,32,512]{2,1,0:T(8,128)} %broadcast_in_dim.7), calls=%async_computation.1 | async-start | bytes 524288 | tf_op jit(solution)/shard_map/all_to_all | solution.py:19
  54.3 23.3 %all-to-all-start.2 = ((f32[8,3,32,512]{3,2,1,0:T(8,128)}), f32[8,3,32,512]{3,2,1,0:T(8,128)}, u32[]{:S(2)}, u32[]{:S(2)}) async-start(f32[8,3,32,512]{3,2,1,0:T(8,128)} %broadcast_in_dim.8), calls=%async_computation.2 | async-start | bytes 3145728 | tf_op jit(solution)/shard_map/all_to_all | solution.py:19
  77.6 25.0 %collective-permute-start.4 = (f32[8,3,32,512]{3,2,1,0:T(8,128)}, f32[8,3,32,512]{3,2,1,0:T(8,128)S(1)}, u32[]{:S(2)}, u32[]{:S(2)}) collective-permute-start(f32[8,3,32,512]{3,2,1,0:T(8,128)} %all-to-all-done.2), channel_id=1, source_target_pairs={{0,1},{1,0},{2,3},{3,2},{4,5},{5,4},{6,7},{7,6},{8,9},{9,8},{10,11... | collective-permute-start | bytes 4718600 | tf_op jit(solution)/shard_map/ppermute | solution.py:23
  81.9 16.8 %collective-permute-start.2 = (f32[32,512]{1,0:T(8,128)S(1)}, f32[32,512]{1,0:T(8,128)S(1)}, u32[]{:S(2)}, u32[]{:S(2)}) collective-permute-start(f32[32,512]{1,0:T(8,128)S(1)} %get-tuple-element.27), channel_id=1, source_target_pairs={{0,32},{16,48},{32,0},{48,16},{1,33},{17,49},{33,1},{49,17},{2,34}... | collective-permute-start | bytes 196616 | tf_op jit(solution)/shard_map/ppermute | solution.py:59
  88.2 10.5 %collective-permute-start.3 = (f32[32,512]{1,0:T(8,128)S(1)}, f32[32,512]{1,0:T(8,128)S(1)}, u32[]{:S(2)}, u32[]{:S(2)}) collective-permute-start(f32[32,512]{1,0:T(8,128)S(1)} %get-tuple-element.26), channel_id=1, source_target_pairs={{0,48},{16,0},{32,16},{48,32},{1,49},{17,1},{33,17},{49,33},{2,50}... | collective-permute-start | bytes 196616 | tf_op jit(solution)/shard_map/ppermute | solution.py:59
  93.7 8.9 %collective-permute-start.1 = (f32[32,512]{1,0:T(8,128)S(1)}, f32[32,512]{1,0:T(8,128)S(1)}, u32[]{:S(2)}, u32[]{:S(2)}) collective-permute-start(f32[32,512]{1,0:T(8,128)S(1)} %get-tuple-element.28), channel_id=1, source_target_pairs={{0,16},{16,32},{32,48},{48,0},{1,17},{17,33},{33,49},{49,1},{2,18}... | collective-permute-start | bytes 196616 | tf_op jit(solution)/shard_map/ppermute | solution.py:59
  107.6 3.9 %collective-permute-start.5 = (f32[32,512]{1,0:T(8,128)S(1)}, f32[32,512]{1,0:T(8,128)S(1)}, u32[]{:S(2)}, u32[]{:S(2)}) collective-permute-start(f32[32,512]{1,0:T(8,128)S(1)} %fusion.5), channel_id=1, source_target_pairs={{448,384},{449,385},{450,386},{451,387},{452,388},{453,389},{454,3... | collective-permute-start | bytes 196616 | tf_op jit(solution)/shard_map/ppermute | solution.py:82
  112.1 1.3 collective-permute-start.6
  114.0 10.9 %collective-permute-start.7 = (f32[32,512]{1,0:T(8,128)S(1)}, f32[32,512]{1,0:T(8,128)S(1)}, u32[]{:S(2)}, u32[]{:S(2)}) collective-permute-start(f32[32,512]{1,0:T(8,128)S(1)} %convolution_add_fusion.8), channel_id=1, source_target_pairs={{320,256},{321,257},{322,258},{323,259},{324,260},{325,261},{326,2... | collective-permute-start | bytes 196616 | tf_op jit(solution)/shard_map/ppermute | solution.py:82
  125.4 3.3 %collective-permute-start.8 = (f32[32,512]{1,0:T(8,128)S(1)}, f32[32,512]{1,0:T(8,128)S(1)}, u32[]{:S(2)}, u32[]{:S(2)}) collective-permute-start(f32[32,512]{1,0:T(8,128)S(1)} %convolution_add_fusion.7), channel_id=1, source_target_pairs={{256,192},{257,193},{258,194},{259,195},{260,196},{261,197},{262,1... | collective-permute-start | bytes 196616 | tf_op jit(solution)/shard_map/ppermute | solution.py:82
  126.8 37.9 %collective-permute-start.12 = (f32[384,512]{1,0:T(8,128)S(1)}, f32[384,512]{1,0:T(8,128)S(1)}, u32[]{:S(2)}, u32[]{:S(2)}) collective-permute-start(f32[384,512]{1,0:T(8,128)S(1)} %pad_maximum_fusion.2), channel_id=1, source_target_pairs={{0,16},{16,32},{32,48},{48,64},{64,80},{80,96},{96,112},{112,128},... | collective-permute-start | bytes 2359304 | tf_op jit(solution)/shard_map/ppermute | solution.py:74
  129.3 0.7 collective-permute-start.9
  130.6 0.7 collective-permute-start.10
  131.9 34.9 %collective-permute-start.11 = (f32[32,512]{1,0:T(8,128)S(1)}, f32[32,512]{1,0:T(8,128)S(1)}, u32[]{:S(2)}, u32[]{:S(2)}) collective-permute-start(f32[32,512]{1,0:T(8,128)S(1)} %convolution_add_fusion.4), channel_id=1, source_target_pairs={{64,0},{65,1},{66,2},{67,3},{68,4},{69,5},{70,6},{71,7},{72,8},{73... | collective-permute-start | bytes 196616 | tf_op jit(solution)/shard_map/ppermute | solution.py:82
  164.8 8.4 %collective-permute-start.13 = (f32[256,512]{1,0:T(8,128)S(1)}, f32[256,512]{1,0:T(8,128)S(1)}, u32[]{:S(2)}, u32[]{:S(2)}) collective-permute-start(f32[256,512]{1,0:T(8,128)S(1)} %slice.84), channel_id=1, source_target_pairs={{0,1},{1,0},{2,3},{3,2},{4,5},{5,4},{6,7},{7,6},{8,9},{9,8},{10,11... | collective-permute-start | bytes 1572872 | tf_op jit(solution)/shard_map/ppermute | solution.py:23
  169.8 14.6 %all-to-all-start.3 = ((f32[4,32,512]{2,1,0:T(8,128)}), f32[4,32,512]{2,1,0:T(8,128)S(1)}, u32[]{:S(2)}, u32[]{:S(2)}) async-start(f32[4,32,512]{2,1,0:T(8,128)} %pad_maximum_fusion.3), calls=%async_computation.3 | async-start | bytes 524288 | tf_op jit(solution)/shard_map/all_to_all | solution.py:89
where the time goes:
time: 187 us; the launch traced here: 186 us
  waiting for transfers between devices  85.2 us (46%)
  starting transfers between devices  42.7 us (23%)
  blocking collectives  25.3 us (14%)
  matrix products  20.7 us (11%)
  other arithmetic  6.83 us (4%)
  local copies, waits for them, and re-layouts  4.58 us (2%)
    ppermute x1, waiting for transfers between devices, transformed(): extra = lax.ppermute(extra, ROW, down)  32.2 us
    all_to_all x1, blocking collectives, spread(): lax.all_to_all(jnp.broadcast_to(part[None], (count, *part.shape)), axes,...  25.3 us
    all_to_all x2, waiting for transfers between devices, spread(): lax.all_to_all(jnp.broadcast_to(part[None], (count, *part.shape)), axes,...  24.9 us
    dot_general x26, matrix products, dot(): lax.dot_general(a, b, (((da,), (db,)), ((), ())), precision=lax.Precision...  20.7 us
    ppermute x3, starting transfers between devices, transformed(): edges.append(lax.ppermute(piece, 'h', above) if s else piece)  13.7 us
    all_to_all x2, starting transfers between devices, spread(): lax.all_to_all(jnp.broadcast_to(part[None], (count, *part.shape)), axes,...  11.9 us
    all_to_all x1, waiting for transfers between devices, transformed(): mine = lax.all_to_all(mine, 'h', 0, 0).reshape(rows * width, band)  11 us
    ppermute x7, waiting for transfers between devices, transformed(): came = lax.ppermute(top, 'z', [(k, k - 1)])  9.55 us
  transfers between devices with their start and end apart: 17, of which 7 were waited for; matrix products, arithmetic and copies ran while one was open for 10% of the time, Pallas kernels for 0%

commit v1 on v0

--- a/solution.py
+++ b/solution.py
@@ -49,6 +49,7 @@
     own = -dot(dot(lax.dynamic_slice_in_dim(upper, here * height, height, 0), triangle, 1, 0), lower, 1, 1)
     shards = spread(own, "h")
     reach = dot(triangle, lower, 1, 1)
+    coupling = lax.optimization_barrier(-dot(upper, reach, 1, 0))
     inner = dot(dot(vectors, upper, 0, 0), triangle, 1, 1)
     edge = vectors.T - dot(inner, upper, 1, 1)
     width = edge.shape[0] // rows
@@ -58,7 +59,6 @@
         above = [(k, (k - s) % rows) for k in range(rows)]
         edges.append(lax.ppermute(piece, "h", above) if s else piece)
     edges = [pick([edges[(k - h) % rows] for h in range(rows)], place) for k in range(rows)]
-    coupling = lax.optimization_barrier(-dot(upper, reach, 1, 0))
     others = [jnp.where(place <= k, shards[k + 1], shards[k]) for k in range(rows - 1)]
     part = spread(jnp.stack(others), ("x", "l"))
     halves = both_halves(part, core, 0).transpose(2, 0, 1, 3, 4).reshape(rows - 1, band, band)
@@ -70,9 +70,10 @@
     down = [(k, k + 1) for k in range(count - 1)]
     pull = dot(lower, reach, 1, 0)
     pull = lax.dynamic_slice_in_dim(pull, core * (band // 2), band // 2, 0)
-    extra = jnp.concatenate([pull, dot(inner, lower, 1, 1)])
+    extra = jnp.concatenate([pull, dot(lower, inner, 1, 1).reshape(-1, band)])
     extra = lax.ppermute(extra, ROW, down)
-    pull, fixed = both_halves(extra[: band // 2], core, 0).reshape(band, band), extra[band // 2 :]
+    pull = both_halves(extra[: band // 2], core, 0).reshape(band, band)
+    fixed = extra[band // 2 :].reshape(band, -1)
     total, bottom = couplings[rows - 1], edges[rows - 1]
     for k in reversed(range(rows - 1)):
         bottom = edges[k] + dot(bottom, couplings[k], 1, 1)
@@ -87,7 +88,7 @@
         tops.insert(0, edges[k] + dot(tops[0], couplings[k], 1, 1))
     mine = jnp.stack([top, *tops[:-1]])
     mine = lax.all_to_all(mine, "h", 0, 0).reshape(rows * width, band)
-    return mine.T - dot(pull, mine, 1, 1) - fixed.T
+    return mine.T - dot(pull, mine, 1, 1) - fixed
 
 
 def solution(mesh):

time: 187 us -> 197 us (1.053)
  the two profiles are of different devices: /device:TPU:258 before, /device:TPU:256 now
where the time goes in v1:
time: 197 us; the launch traced here: 196 us
  waiting for transfers between devices  82.7 us (42%)
  starting transfers between devices  42.3 us (21%)
  blocking collectives  26.6 us (14%)
  matrix products  26.6 us (14%)
  local copies, waits for them, and re-layouts  8.69 us (4%)
  other arithmetic  7.93 us (4%)
    ppermute x1, waiting for transfers between devices, transformed(): extra = lax.ppermute(extra, ROW, down)  31.4 us
    all_to_all x1, blocking collectives, spread(): lax.all_to_all(jnp.broadcast_to(part[None], (count, *part.shape)), axes,...  26.6 us
    dot_general x26, matrix products, dot(): lax.dot_general(a, b, (((da,), (db,)), ((), ())), precision=lax.Precision...  26.6 us
    all_to_all x2, waiting for transfers between devices, spread(): lax.all_to_all(jnp.broadcast_to(part[None], (count, *part.shape)), axes,...  26.4 us
    ppermute x3, starting transfers between devices, transformed(): edges.append(lax.ppermute(piece, 'h', above) if s else piece)  13.4 us
    all_to_all x2, starting transfers between devices, spread(): lax.all_to_all(jnp.broadcast_to(part[None], (count, *part.shape)), axes,...  10.5 us
    all_to_all x1, waiting for transfers between devices, transformed(): mine = lax.all_to_all(mine, 'h', 0, 0).reshape(rows * width, band)  9.95 us
    ppermute x7, waiting for transfers between devices, transformed(): came = lax.ppermute(top, 'z', [(k, k - 1)])  8.21 us
  transfers between devices with their start and end apart: 17, of which 7 were waited for; matrix products, arithmetic and copies ran while one was open for 13% of the time, Pallas kernels for 0%

profile of v1, /device:TPU:256, one launch (start us, length us, event | category | flops | bytes accessed | tf_op | source)
XLA Modules:
  0.0 195.6 jit_solution(369463336355713866)
XLA Ops:
  1.2 26.6 %all_to_all.20 = f32[8,96,512]{2,1,0:T(8,128)S(1)} all-to-all(f32[8,96,512]{2,1,0:T(8,128)S(1)} %broadcast_in_dim.6), channel_id=1, replica_groups=mesh['z'=8,'h'=4,'x'=4,'l'=2,'c'=2] {'x','l'}, dimensions={0} | all-to-all | bytes 3145728 | tf_op jit(solution)/shard_map/all_to_all | solution.py:19
  27.8 1.9 collective-permute-start
  29.7 3.5 %collective-permute-done = f32[8,96,512]{2,1,0:T(8,128)} collective-permute-done((f32[8,96,512]{2,1,0:T(8,128)S(1)}, f32[8,96,512]{2,1,0:T(8,128)}, u32[]{:S(2)}, u32[]{:S(2)}) %collective-permute-start) | collective-permute-done | bytes 1572896 | tf_op jit(solution)/shard_map/ppermute | solution.py:23
  33.2 1.8 select_bitcast_fusion.3
  37.0 6.2 %all-to-all-start.1 = ((f32[4,32,512]{2,1,0:T(8,128)}), f32[4,32,512]{2,1,0:T(8,128)S(1)}, u32[]{:S(2)}, u32[]{:S(2)}) async-start(f32[4,32,512]{2,1,0:T(8,128)} %broadcast_in_dim.7), calls=%async_computation.1 | async-start | bytes 524288 | tf_op jit(solution)/shard_map/all_to_all | solution.py:19
  43.2 10.7 %all-to-all-done.1 = f32[4,32,512]{2,1,0:T(8,128)S(1)} async-done(((f32[4,32,512]{2,1,0:T(8,128)}), f32[4,32,512]{2,1,0:T(8,128)S(1)}, u32[]{:S(2)}, u32[]{:S(2)}) %all-to-all-start.1) | async-done | bytes 262176 | tf_op jit(solution)/shard_map/all_to_all | solution.py:19
  55.3 4.3 %all-to-all-start.2 = ((f32[8,3,32,512]{3,2,1,0:T(8,128)}), f32[8,3,32,512]{3,2,1,0:T(8,128)}, u32[]{:S(2)}, u32[]{:S(2)}) async-start(f32[8,3,32,512]{3,2,1,0:T(8,128)} %broadcast_in_dim.8), calls=%async_computation.2 | async-start | bytes 3145728 | tf_op jit(solution)/shard_map/all_to_all | solution.py:19
  60.7 2.7 %fusion.21 = f32[512,128]{1,0:T(8,128)} fusion(f32[512,512]{1,0:T(8,128)S(1)} %bitcast.127, f32[512,128]{1,0:T(8,128)} %param.3), kind=kOutput, calls=%fused_computation.71 | convolution fusion | flops 201326592 | bytes 1572864 | tf_op jit(solution)/shard_map/dot_general | solution.py:12
  63.4 15.7 %all-to-all-done.2 = f32[8,3,32,512]{3,2,1,0:T(8,128)} async-done(((f32[8,3,32,512]{3,2,1,0:T(8,128)}), f32[8,3,32,512]{3,2,1,0:T(8,128)}, u32[]{:S(2)}, u32[]{:S(2)}) %all-to-all-start.2) | async-done | bytes 1572896 | tf_op jit(solution)/shard_map/all_to_all | solution.py:19
  79.1 1.9 collective-permute-start.4
  83.4 4.9 %collective-permute-start.3 = (f32[32,512]{1,0:T(8,128)S(1)}, f32[32,512]{1,0:T(8,128)S(1)}, u32[]{:S(2)}, u32[]{:S(2)}) collective-permute-start(f32[32,512]{1,0:T(8,128)S(1)} %get-tuple-element.26), channel_id=1, source_target_pairs={{0,48},{16,0},{32,16},{48,32},{1,49},{17,1},{33,17},{49,33},{2,50}... | collective-permute-start | bytes 196616 | tf_op jit(solution)/shard_map/ppermute | solution.py:60
  88.3 6.6 %collective-permute-start.2 = (f32[32,512]{1,0:T(8,128)S(1)}, f32[32,512]{1,0:T(8,128)S(1)}, u32[]{:S(2)}, u32[]{:S(2)}) collective-permute-start(f32[32,512]{1,0:T(8,128)S(1)} %get-tuple-element.27), channel_id=1, source_target_pairs={{0,32},{16,48},{32,0},{48,16},{1,33},{17,49},{33,1},{49,17},{2,34}... | collective-permute-start | bytes 196616 | tf_op jit(solution)/shard_map/ppermute | solution.py:60
  94.9 1.9 collective-permute-start.1
  98.9 2.0 %fusion.27 = f32[512,512]{1,0:T(8,128)} fusion(f32[512,512]{1,0:T(8,128)S(1)} %bitcast.124, f32[512,512]{1,0:T(8,128)S(1)} %fusion.23), kind=kOutput, calls=%fused_computation.77 | convolution fusion | flops 805306368 | bytes 3145728 | tf_op jit(solution)/shard_map/dot_general | solution.py:12
  100.9 3.1 %collective-permute-done.1 = f32[32,512]{1,0:T(8,128)S(1)} collective-permute-done((f32[32,512]{1,0:T(8,128)S(1)}, f32[32,512]{1,0:T(8,128)S(1)}, u32[]{:S(2)}, u32[]{:S(2)}) %collective-permute-start.1) | collective-permute-done | bytes 65568 | tf_op jit(solution)/shard_map/ppermute | solution.py:60
  104.1 1.9 select_bitcast_fusion.1
  120.2 8.2 %collective-permute-done.7 = f32[32,512]{1,0:T(8,128)S(1)} collective-permute-done((f32[32,512]{1,0:T(8,128)S(1)}, f32[32,512]{1,0:T(8,128)S(1)}, u32[]{:S(2)}, u32[]{:S(2)}) %collective-permute-start.7) | collective-permute-done | bytes 65568 | tf_op jit(solution)/shard_map/ppermute | solution.py:83
  130.3 1.9 collective-permute-start.12
  137.4 31.4 %collective-permute-done.12 = f32[384,512]{1,0:T(8,128)S(1)} collective-permute-done((f32[384,512]{1,0:T(8,128)S(1)}, f32[384,512]{1,0:T(8,128)S(1)}, u32[]{:S(2)}, u32[]{:S(2)}) %collective-permute-start.12) | collective-permute-done | bytes 786464 | tf_op jit(solution)/shard_map/ppermute | solution.py:74
  170.5 1.9 slice.84
  172.3 1.9 collective-permute-start.13
  174.2 1.9 convolution_add_fusion.2
  179.5 3.4 %all-to-all-start.3 = ((f32[4,32,512]{2,1,0:T(8,128)}), f32[4,32,512]{2,1,0:T(8,128)S(1)}, u32[]{:S(2)}, u32[]{:S(2)}) async-start(f32[4,32,512]{2,1,0:T(8,128)} %pad_maximum_fusion.3), calls=%async_computation.3 | async-start | bytes 524288 | tf_op jit(solution)/shard_map/all_to_all | solution.py:90
  184.2 10.0 %all-to-all-done.3 = f32[4,32,512]{2,1,0:T(8,128)S(1)} async-done(((f32[4,32,512]{2,1,0:T(8,128)}), f32[4,32,512]{2,1,0:T(8,128)S(1)}, u32[]{:S(2)}, u32[]{:S(2)}) %all-to-all-start.3) | async-done | bytes 262176 | tf_op jit(solution)/shard_map/all_to_all | solution.py:90
  (87 shorter events, 38.5 us)
Async XLA Ops:
  27.8 5.4 %collective-permute-start = (f32[8,96,512]{2,1,0:T(8,128)S(1)}, f32[8,96,512]{2,1,0:T(8,128)}, u32[]{:S(2)}, u32[]{:S(2)}) collective-permute-start(f32[8,96,512]{2,1,0:T(8,128)S(1)} %all_to_all.20), channel_id=1, source_target_pairs={{0,1},{1,0},{2,3},{3,2},{4,5},{5,4},{6,7},{7,6},{8,9},{9,8},{10,11... | collective-permute-start | bytes 4718600 | tf_op jit(solution)/shard_map/ppermute | solution.py:23
  37.0 16.9 %all-to-all-start.1 = ((f32[4,32,512]{2,1,0:T(8,128)}), f32[4,32,512]{2,1,0:T(8,128)S(1)}, u32[]{:S(2)}, u32[]{:S(2)}) async-start(f32[4,32,512]{2,1,0:T(8,128)} %broadcast_in_dim.7), calls=%async_computation.1 | async-start | bytes 524288 | tf_op jit(solution)/shard_map/all_to_all | solution.py:19
  55.3 23.9 %all-to-all-start.2 = ((f32[8,3,32,512]{3,2,1,0:T(8,128)}), f32[8,3,32,512]{3,2,1,0:T(8,128)}, u32[]{:S(2)}, u32[]{:S(2)}) async-start(f32[8,3,32,512]{3,2,1,0:T(8,128)} %broadcast_in_dim.8), calls=%async_computation.2 | async-start | bytes 3145728 | tf_op jit(solution)/shard_map/all_to_all | solution.py:19
  79.1 24.9 %collective-permute-start.4 = (f32[8,3,32,512]{3,2,1,0:T(8,128)}, f32[8,3,32,512]{3,2,1,0:T(8,128)S(1)}, u32[]{:S(2)}, u32[]{:S(2)}) collective-permute-start(f32[8,3,32,512]{3,2,1,0:T(8,128)} %all-to-all-done.2), channel_id=1, source_target_pairs={{0,1},{1,0},{2,3},{3,2},{4,5},{5,4},{6,7},{7,6},{8,9},{9,8},{10,11... | collective-permute-start | bytes 4718600 | tf_op jit(solution)/shard_map/ppermute | solution.py:23
  83.4 17.5 %collective-permute-start.3 = (f32[32,512]{1,0:T(8,128)S(1)}, f32[32,512]{1,0:T(8,128)S(1)}, u32[]{:S(2)}, u32[]{:S(2)}) collective-permute-start(f32[32,512]{1,0:T(8,128)S(1)} %get-tuple-element.26), channel_id=1, source_target_pairs={{0,48},{16,0},{32,16},{48,32},{1,49},{17,1},{33,17},{49,33},{2,50}... | collective-permute-start | bytes 196616 | tf_op jit(solution)/shard_map/ppermute | solution.py:60
  88.3 12.6 %collective-permute-start.2 = (f32[32,512]{1,0:T(8,128)S(1)}, f32[32,512]{1,0:T(8,128)S(1)}, u32[]{:S(2)}, u32[]{:S(2)}) collective-permute-start(f32[32,512]{1,0:T(8,128)S(1)} %get-tuple-element.27), channel_id=1, source_target_pairs={{0,32},{16,48},{32,0},{48,16},{1,33},{17,49},{33,1},{49,17},{2,34}... | collective-permute-start | bytes 196616 | tf_op jit(solution)/shard_map/ppermute | solution.py:60
  94.9 9.1 %collective-permute-start.1 = (f32[32,512]{1,0:T(8,128)S(1)}, f32[32,512]{1,0:T(8,128)S(1)}, u32[]{:S(2)}, u32[]{:S(2)}) collective-permute-start(f32[32,512]{1,0:T(8,128)S(1)} %get-tuple-element.28), channel_id=1, source_target_pairs={{0,16},{16,32},{32,48},{48,0},{1,17},{17,33},{33,49},{49,1},{2,18}... | collective-permute-start | bytes 196616 | tf_op jit(solution)/shard_map/ppermute | solution.py:60
  109.3 3.9 %collective-permute-start.5 = (f32[32,512]{1,0:T(8,128)S(1)}, f32[32,512]{1,0:T(8,128)S(1)}, u32[]{:S(2)}, u32[]{:S(2)}) collective-permute-start(f32[32,512]{1,0:T(8,128)S(1)} %fusion.5), channel_id=1, source_target_pairs={{448,384},{449,385},{450,386},{451,387},{452,388},{453,389},{454,3... | collective-permute-start | bytes 196616 | tf_op jit(solution)/shard_map/ppermute | solution.py:83
  114.4 1.9 collective-permute-start.6
  117.8 10.6 %collective-permute-start.7 = (f32[32,512]{1,0:T(8,128)S(1)}, f32[32,512]{1,0:T(8,128)S(1)}, u32[]{:S(2)}, u32[]{:S(2)}) collective-permute-start(f32[32,512]{1,0:T(8,128)S(1)} %convolution_add_fusion.8), channel_id=1, source_target_pairs={{320,256},{321,257},{322,258},{323,259},{324,260},{325,261},{326,2... | collective-permute-start | bytes 196616 | tf_op jit(solution)/shard_map/ppermute | solution.py:83
  128.4 4.5 %copy-start.8 = (f32[32,512]{1,0:T(8,128)}, f32[32,512]{1,0:T(8,128)S(1)}, u32[]{:S(2)}) copy-start(f32[32,512]{1,0:T(8,128)S(1)} %collective-permute-done.7) | copy-start | bytes 196612
  129.0 3.3 %collective-permute-start.8 = (f32[32,512]{1,0:T(8,128)S(1)}, f32[32,512]{1,0:T(8,128)S(1)}, u32[]{:S(2)}, u32[]{:S(2)}) collective-permute-start(f32[32,512]{1,0:T(8,128)S(1)} %convolution_add_fusion.7), channel_id=1, source_target_pairs={{256,192},{257,193},{258,194},{259,195},{260,196},{261,197},{262,1... | collective-permute-start | bytes 196616 | tf_op jit(solution)/shard_map/ppermute | solution.py:83
  130.3 38.4 %collective-permute-start.12 = (f32[384,512]{1,0:T(8,128)S(1)}, f32[384,512]{1,0:T(8,128)S(1)}, u32[]{:S(2)}, u32[]{:S(2)}) collective-permute-start(f32[384,512]{1,0:T(8,128)S(1)} %pad_maximum_fusion.2), channel_id=1, source_target_pairs={{0,16},{16,32},{32,48},{48,64},{64,80},{80,96},{96,112},{112,128},... | collective-permute-start | bytes 2359304 | tf_op jit(solution)/shard_map/ppermute | solution.py:74
  132.3 3.8 %copy-start.9 = (f32[32,512]{1,0:T(8,128)}, f32[32,512]{1,0:T(8,128)S(1)}, u32[]{:S(2)}) copy-start(f32[32,512]{1,0:T(8,128)S(1)} %collective-permute-done.8) | copy-start | bytes 196612
  132.9 0.7 collective-permute-start.9
  133.6 35.2 %copy-start.10 = (f32[32,512]{1,0:T(8,128)}, f32[32,512]{1,0:T(8,128)S(1)}, u32[]{:S(2)}) copy-start(f32[32,512]{1,0:T(8,128)S(1)} %collective-permute-done.9) | copy-start | bytes 196612
  134.2 0.7 collective-permute-start.10
  134.8 34.0 %copy-start.11 = (f32[32,512]{1,0:T(8,128)}, f32[32,512]{1,0:T(8,128)S(1)}, u32[]{:S(2)}) copy-start(f32[32,512]{1,0:T(8,128)S(1)} %collective-permute-done.10) | copy-start | bytes 196612
  136.1 38.2 %collective-permute-start.11 = (f32[32,512]{1,0:T(8,128)}, f32[32,512]{1,0:T(8,128)}, u32[]{:S(2)}, u32[]{:S(2)}) collective-permute-start(f32[32,512]{1,0:T(8,128)} %convolution_add_fusion.4), channel_id=1, source_target_pairs={{64,0},{65,1},{66,2},{67,3},{68,4},{69,5},{70,6},{71,7},{72,8},{73... | collective-permute-start | bytes 196616 | tf_op jit(solution)/shard_map/ppermute | solution.py:83
  169.7 6.4 %copy-start.1 = (f32[512,512]{1,0:T(8,128)S(1)}, f32[512,512]{1,0:T(8,128)}, u32[]{:S(2)}) copy-start(f32[512,512]{1,0:T(8,128)} %copy-done) | copy-start | bytes 3145732
  172.3 10.6 %collective-permute-start.13 = (f32[256,512]{1,0:T(8,128)}, f32[256,512]{1,0:T(8,128)}, u32[]{:S(2)}, u32[]{:S(2)}) collective-permute-start(f32[256,512]{1,0:T(8,128)} %slice.84), channel_id=1, source_target_pairs={{0,1},{1,0},{2,3},{3,2},{4,5},{5,4},{6,7},{7,6},{8,9},{9,8},{10,11... | collective-permute-start | bytes 1572872 | tf_op jit(solution)/shard_map/ppermute | solution.py:23
  176.8 6.2 %copy-start.4 = (f32[384,512]{1,0:T(8,128)S(1)}, f32[384,512]{1,0:T(8,128)}, u32[]{:S(2)}) copy-start(f32[384,512]{1,0:T(8,128)} %copy-done.3) | copy-start | bytes 2359300
  179.5 14.6 %all-to-all-start.3 = ((f32[4,32,512]{2,1,0:T(8,128)}), f32[4,32,512]{2,1,0:T(8,128)S(1)}, u32[]{:S(2)}, u32[]{:S(2)}) async-start(f32[4,32,512]{2,1,0:T(8,128)} %pad_maximum_fusion.3), calls=%async_computation.3 | async-start | bytes 524288 | tf_op jit(solution)/shard_map/all_to_all | solution.py:90
  184.1 10.2 %copy-start.5 = (f32[512,128]{1,0:T(8,128)S(1)}, f32[512,128]{1,0:T(8,128)}, u32[]{:S(2)}) copy-start(f32[512,128]{1,0:T(8,128)} %reshape.36) | copy-start | bytes 786436
  (5 other events, 10.9 us)
